TPU v7x, 256 devices: a whole 4x4x8 slice. The times are simulated.
256 devices in a mesh: dp: 16 (over x, y_hi, core), fsdp: 16 (over y_lo, z).
Axes of the slice: x: 4, y: 4 (y_hi: 2, y_lo: 2; y = y_hi * 2 + y_lo), z: 8, core: 2. Of those that a mesh axis runs over, the one named last changes fastest.
Arguments:
- tokens: bfloat16 [8192, 2048], P('dp'), may hold values from -6 to 6
- expert_ids: int32 [8192, 2], P('dp'), may hold values from 0 to 7, as said below
- route_probs: float32 [8192, 2], P('dp'), may hold values from 0.1 to 1
- gate_w: bfloat16 [2, 2048, 7168], P(None, 'dp', 'fsdp'), may hold values from -0.125 to 0.125
- up_w: bfloat16 [2, 2048, 7168], P(None, 'dp', 'fsdp'), may hold values from -0.125 to 0.125
- down_w: bfloat16 [2, 7168, 2048], P(None, 'fsdp', 'dp'), may hold values from -0.0625 to 0.0625
- out_grad: bfloat16 [8192, 2048], P('dp'), may hold values from -6 to 6
Outputs:
- mixed: bfloat16 [8192, 2048], P('dp')
- token_grad: bfloat16 [8192, 2048], P('dp')
- gate_grad: bfloat16 [2, 2048, 7168], P(None, 'dp', 'fsdp')
- up_grad: bfloat16 [2, 2048, 7168], P(None, 'dp', 'fsdp')
- down_grad: bfloat16 [2, 7168, 2048], P(None, 'fsdp', 'dp')
Inputs may be any that keep to these rules, and one draw needn't show every extreme that they name: `expert_ids`: the two entries of a row differ. In each aligned block of 512 rows (the rows of one index of dp) every expert is named by at most 256 rows, and one of experts 0 to 1 by exactly 256 rows.
All inputs are finite; a program needn't handle non-finite values.
Results may differ from a plain program's by a relative error of at most 0.018.
Values may be sent and summed in bfloat16 or wider, within the bound.
A program may use at most 128 MiB of HBM per device.

v0:
```python
import jax
import jax.numpy as jnp
from jax import lax
from jax.sharding import PartitionSpec as P


def slot_layout(expert_ids, route_probs, expert, slot_cap):
    token_count = expert_ids.shape[0]
    matches = expert_ids == expert
    chosen = jnp.any(matches, axis=1)
    weight_token = jnp.sum(jnp.where(matches, route_probs, jnp.float32(0.0)), axis=1)
    position = jnp.cumsum(chosen.astype(jnp.int32)) - 1
    slot_index = lax.broadcasted_iota(jnp.int32, (slot_cap, token_count), 0)
    token_index = lax.broadcasted_iota(jnp.int32, (slot_cap, token_count), 1)
    matched_slots = (position[None, :] == slot_index) & chosen[None, :]
    slot_token = jnp.sum(jnp.where(matched_slots, token_index, 0), axis=1)
    slot_valid = jnp.any(matched_slots, axis=1)
    slot_weight = jnp.where(slot_valid, jnp.take(weight_token, slot_token), jnp.float32(0.0))
    token_slot = jnp.clip(position, 0, slot_cap - 1)
    return (chosen, token_slot, slot_token, slot_valid, slot_weight)


def group_total(partial_value):
    return lax.psum(partial_value.astype(jnp.bfloat16), "fsdp")


def body(tokens, expert_ids, route_probs, gate_w, up_w, down_w, out_grad):
    token_count = tokens.shape[0]
    width = tokens.shape[1]
    slot_cap = token_count // 2
    window = gate_w.shape[0]
    mixed_part = jnp.zeros((token_count, width), jnp.float32)
    stored = []
    for expert in range(window):
        chosen, token_slot, slot_token, slot_valid, slot_weight = slot_layout(
            expert_ids, route_probs, expert, slot_cap
        )
        gate_full, up_full, down_full = (
            lax.all_gather(gate_w[expert], "dp", axis=0, tiled=True),
            lax.all_gather(up_w[expert], "dp", axis=0, tiled=True),
            lax.all_gather(down_w[expert], "dp", axis=1, tiled=True),
        )
        slot_input = jnp.take(tokens, slot_token, axis=0) * slot_valid[:, None].astype(tokens.dtype)
        gate_act = jnp.dot(slot_input, gate_full, preferred_element_type=jnp.float32)
        up_act = jnp.dot(slot_input, up_full, preferred_element_type=jnp.float32)
        hidden = (jax.nn.silu(gate_act) * up_act).astype(jnp.bfloat16)
        expert_out = (
            jnp.dot(hidden, down_full, preferred_element_type=jnp.float32) * slot_weight[:, None]
        )
        mixed_part = mixed_part + jnp.where(
            chosen[:, None], jnp.take(expert_out, token_slot, axis=0), jnp.float32(0.0)
        )
        stored.append(
            (
                chosen,
                token_slot,
                slot_token,
                slot_weight,
                slot_input,
                gate_act,
                up_act,
                hidden,
                gate_full,
                up_full,
                down_full,
            )
        )
    mixed = group_total(mixed_part)
    grad_part = jnp.zeros((token_count, width), jnp.float32)
    gate_grads, up_grads, down_grads = ([], [], [])
    for expert in range(window):
        (
            chosen,
            token_slot,
            slot_token,
            slot_weight,
            slot_input,
            gate_act,
            up_act,
            hidden,
            gate_full,
            up_full,
            down_full,
        ) = stored[expert]
        slot_grad = (
            jnp.take(out_grad, slot_token, axis=0).astype(jnp.float32) * slot_weight[:, None]
        ).astype(jnp.bfloat16)
        down_term = lax.dot_general(
            hidden, slot_grad, (((0,), (0,)), ((), ())), preferred_element_type=jnp.float32
        )
        hidden_grad = lax.dot_general(
            slot_grad, down_full, (((1,), (1,)), ((), ())), preferred_element_type=jnp.float32
        )
        sigma = jax.nn.sigmoid(gate_act)
        up_act_grad = (hidden_grad * gate_act * sigma).astype(jnp.bfloat16)
        gate_act_grad = (hidden_grad * up_act * sigma * (1.0 + gate_act * (1.0 - sigma))).astype(
            jnp.bfloat16
        )
        gate_term = lax.dot_general(
            slot_input, gate_act_grad, (((0,), (0,)), ((), ())), preferred_element_type=jnp.float32
        )
        up_term = lax.dot_general(
            slot_input, up_act_grad, (((0,), (0,)), ((), ())), preferred_element_type=jnp.float32
        )
        input_grad = lax.dot_general(
            gate_act_grad, gate_full, (((1,), (1,)), ((), ())), preferred_element_type=jnp.float32
        )
        input_grad = input_grad + lax.dot_general(
            up_act_grad, up_full, (((1,), (1,)), ((), ())), preferred_element_type=jnp.float32
        )
        grad_part = grad_part + jnp.where(
            chosen[:, None], jnp.take(input_grad, token_slot, axis=0), jnp.float32(0.0)
        )
        gate_sum, up_sum, down_sum = (
            lax.psum_scatter(
                gate_term.astype(jnp.bfloat16), "dp", scatter_dimension=0, tiled=True
            ).astype(jnp.float32),
            lax.psum_scatter(
                up_term.astype(jnp.bfloat16), "dp", scatter_dimension=0, tiled=True
            ).astype(jnp.float32),
            lax.psum_scatter(
                down_term.astype(jnp.bfloat16), "dp", scatter_dimension=1, tiled=True
            ).astype(jnp.float32),
        )
        gate_grads.append(gate_sum.astype(jnp.bfloat16))
        up_grads.append(up_sum.astype(jnp.bfloat16))
        down_grads.append(down_sum.astype(jnp.bfloat16))
    gate_grad = jnp.stack(gate_grads)
    up_grad = jnp.stack(up_grads)
    down_grad = jnp.stack(down_grads)
    token_grad = group_total(grad_part)
    return (mixed, token_grad, gate_grad, up_grad, down_grad)


def solution(mesh):
    placed = (
        P("dp", None),
        P("dp", None),
        P("dp", None),
        P(None, "dp", "fsdp"),
        P(None, "dp", "fsdp"),
        P(None, "fsdp", "dp"),
        P("dp", None),
    )
    return jax.shard_map(
        body,
        mesh=mesh,
        in_specs=placed,
        out_specs=(
            P("dp", None),
            P("dp", None),
            P(None, "dp", "fsdp"),
            P(None, "dp", "fsdp"),
            P(None, "fsdp", "dp"),
        ),
        check_vma=False,
    )
```

profile of v0, /device:TPU:4, one launch (start us, length us, event | category | flops | bytes accessed | tf_op | source)
XLA Modules:
  0.0 1003.4 jit_solution(5504983384310768062)
XLA Ops:
  7.2 1.8 fusion.32
  9.1 1.7 fusion.31
  10.8 1.7 fusion.30
  16.1 1.9 gather_fusion.4
  18.1 1.4 gather_fusion.3
  19.5 5.2 gather_fusion.8
  24.7 41.6 %all-gather.21.cloned.1.call-done = bf16[1,2048,448]{1,2,0:T(8,128)(2,1)} async-done(((bf16[1,128,448]{1,2,0:T(8,128)(2,1)}), bf16[1,2048,448]{1,2,0:T(8,128)(2,1)}) %all-gather.21.cloned.1.call-update) | async-done | bytes 1835024 | tf_op jit(solution)/shard_map/all_gather | solution.py:40
  66.2 3.1 fusion.8
  69.3 52.5 %all-gather.19.cloned.1.call-done = bf16[1,2048,448]{1,2,0:T(8,128)(2,1)} async-done(((bf16[1,128,448]{1,2,0:T(8,128)(2,1)}), bf16[1,2048,448]{1,2,0:T(8,128)(2,1)}) %all-gather.19.cloned.1.call-update) | async-done | bytes 1835024 | tf_op jit(solution)/shard_map/all_gather | solution.py:39
  121.8 3.0 fusion.12
  124.9 52.0 %all-gather.23.cloned.1.call-done = bf16[1,448,2048]{2,1,0:T(8,128)(2,1)} async-done(((bf16[1,448,128]{2,1,0:T(8,128)(2,1)}), bf16[1,448,2048]{2,1,0:T(8,128)(2,1)}) %all-gather.23.cloned.1.call-update) | async-done | bytes 1835024 | tf_op jit(solution)/shard_map/all_gather | solution.py:41
  176.9 3.7 multiply_convert_fusion.2
  180.5 0.7 copy-done.10
  181.2 2.0 convolution_convert_fusion.4
  183.2 3.8 copy.22
  187.3 2.3 gather_fusion
  189.6 4.3 gather_fusion.6
  194.1 1.9 gather_fusion.1
  196.1 36.2 %all-gather.15.cloned.1.call-done = bf16[1,2048,448]{1,2,0:T(8,128)(2,1)} async-done(((bf16[1,128,448]{1,2,0:T(8,128)(2,1)}), bf16[1,2048,448]{1,2,0:T(8,128)(2,1)}) %all-gather.15.cloned.1.call-update) | async-done | bytes 1835024 | tf_op jit(solution)/shard_map/all_gather | solution.py:40
  232.3 3.0 fusion.18
  235.4 52.4 %all-gather.13.cloned.1.call-done = bf16[1,2048,448]{1,2,0:T(8,128)(2,1)} async-done(((bf16[1,128,448]{1,2,0:T(8,128)(2,1)}), bf16[1,2048,448]{1,2,0:T(8,128)(2,1)}) %all-gather.13.cloned.1.call-update) | async-done | bytes 1835024 | tf_op jit(solution)/shard_map/all_gather | solution.py:39
  287.8 3.1 fusion.22
  290.9 51.8 %all-gather.17.cloned.1.call-done = bf16[1,448,2048]{2,1,0:T(8,128)(2,1)} async-done(((bf16[1,448,128]{2,1,0:T(8,128)(2,1)}), bf16[1,448,2048]{2,1,0:T(8,128)(2,1)}) %all-gather.17.cloned.1.call-update) | async-done | bytes 1835024 | tf_op jit(solution)/shard_map/all_gather | solution.py:41
  342.7 3.3 multiply_convert_fusion.4
  346.0 0.7 copy-done.16
  346.7 2.0 convolution_convert_fusion.5
  348.7 2.4 copy.20
  351.2 2.0 convolution_convert_fusion.1
  353.2 2.5 copy.16
  355.8 2.0 convolution_convert_fusion.3
  357.8 2.4 copy.12
  360.3 0.8 convolution_convert_fusion
  361.1 2.5 copy.18
  363.7 0.8 convolution_convert_fusion.2
  364.5 2.4 copy.14
  367.2 2.3 convolution_multiply_fusion.1
  369.5 3.6 gather_fusion.2
  373.1 2.4 fusion.20
  375.5 0.7 convolution_add_fusion.1
  376.3 3.6 gather_fusion.7
  379.9 2.2 convolution_multiply_fusion
  382.2 3.6 gather_fusion.5
  385.8 2.4 fusion.10
  388.1 0.7 convolution_add_fusion
  388.9 3.6 gather_fusion.9
  392.4 9.4 fusion.1
  401.9 22.4 %reduce-scatter.29.cloned.1.call-done = bf16[128,448]{1,0:T(8,128)(2,1)} async-done(((bf16[2048,448]{1,0:T(8,128)(2,1)}), bf16[128,448]{1,0:T(8,128)(2,1)}) %reduce-scatter.29.cloned.1.call-update) | async-done | bytes 114704
  424.3 1.0 copy.23
  425.3 80.9 %reduce-scatter.27.cloned.1.call-done = bf16[128,448]{1,0:T(8,128)(2,1)} async-done(((bf16[2048,448]{1,0:T(8,128)(2,1)}), bf16[128,448]{1,0:T(8,128)(2,1)}) %reduce-scatter.27.cloned.1.call-update) | async-done | bytes 114704
  506.3 1.0 copy.21
  507.3 80.9 %reduce-scatter.23.cloned.1.call-done = bf16[128,448]{1,0:T(8,128)(2,1)} async-done(((bf16[2048,448]{1,0:T(8,128)(2,1)}), bf16[128,448]{1,0:T(8,128)(2,1)}) %reduce-scatter.23.cloned.1.call-update) | async-done | bytes 114704
  588.3 1.0 copy.17
  589.3 80.8 %reduce-scatter.19.cloned.1.call-done = bf16[128,448]{1,0:T(8,128)(2,1)} async-done(((bf16[2048,448]{1,0:T(8,128)(2,1)}), bf16[128,448]{1,0:T(8,128)(2,1)}) %reduce-scatter.19.cloned.1.call-update) | async-done | bytes 114704
  670.1 1.0 copy.13
  671.1 81.0 %reduce-scatter.25.cloned.1.call-done = bf16[128,448]{1,0:T(8,128)(2,1)} async-done(((bf16[2048,448]{1,0:T(8,128)(2,1)}), bf16[128,448]{1,0:T(8,128)(2,1)}) %reduce-scatter.25.cloned.1.call-update) | async-done | bytes 114704
  752.1 1.0 copy.19
  753.1 80.8 %reduce-scatter.21.cloned.1.call-done = bf16[128,448]{1,0:T(8,128)(2,1)} async-done(((bf16[2048,448]{1,0:T(8,128)(2,1)}), bf16[128,448]{1,0:T(8,128)(2,1)}) %reduce-scatter.21.cloned.1.call-update) | async-done | bytes 114704
  833.9 1.0 copy.15
  835.0 0.7 pad_maximum_fusion.2
  835.7 0.7 pad_maximum_fusion.1
  836.4 0.7 pad_maximum_fusion
  837.1 155.1 %all-reduce.3.cloned.1.call-done = (bf16[512,2048]{1,0:T(8,128)(2,1)}, bf16[512,2048]{1,0:T(8,128)(2,1)}) async-done(((bf16[512,2048]{1,0:T(8,128)(2,1)}, bf16[512,2048]{1,0:T(8,128)(2,1)}), (bf16[512,2048]{1,0:T(8,128)(2,1)}, bf16[512,2048]{1,0:T(8,128)(2,1)})) %all-reduce.3.cloned.1.call-update) | async-done | bytes 4194320 | tf_op jit(solution)/shard_map/psum | solution.py:24
  992.2 3.3 copy.26
  995.5 1.3 copy.27
  (93 shorter events, 4.7 us)
Async XLA Ops:
  7.2 10.9 %copy-start = (bf16[512,2048]{1,0:T(8,128)(2,1)S(1)}, bf16[512,2048]{1,0:T(8,128)(2,1)}, u32[]{:S(2)}) copy-start(bf16[512,2048]{1,0:T(8,128)(2,1)} %param.13) | copy-start | bytes 6291460
  7.2 7.1 copy-start.18
  7.2 8.9 copy-start.19
  7.2 59.0 %all-gather.21.cloned.1.call-start = ((), (), s32[]{:S(2)}) async-start(), calls=%async_computation.10 | async-start | bytes 1949696 | tf_op jit(solution)/shard_map/all_gather | solution.py:40
  9.1 112.8 %all-gather.19.cloned.1.call-start = ((), (), s32[]{:S(2)}) async-start(), calls=%async_computation.9 | async-start | bytes 1949696 | tf_op jit(solution)/shard_map/all_gather | solution.py:39
  10.8 166.1 %all-gather.23.cloned.1.call-start = ((), (), s32[]{:S(2)}) async-start(), calls=%async_computation.11 | async-start | bytes 1949696 | tf_op jit(solution)/shard_map/all_gather | solution.py:41
  12.5 219.8 %all-gather.15.cloned.1.call-start = ((), (), s32[]{:S(2)}) async-start(), calls=%async_computation.7 | async-start | bytes 1949696 | tf_op jit(solution)/shard_map/all_gather | solution.py:40
  13.1 274.7 %all-gather.13.cloned.1.call-start = ((), (), s32[]{:S(2)}) async-start(), calls=%async_computation.6 | async-start | bytes 1949696 | tf_op jit(solution)/shard_map/all_gather | solution.py:39
  13.7 329.0 %all-gather.17.cloned.1.call-start = ((), (), s32[]{:S(2)}) async-start(), calls=%async_computation.8 | async-start | bytes 1949696 | tf_op jit(solution)/shard_map/all_gather | solution.py:41
  14.3 410.0 %reduce-scatter.29.cloned.1.call-start = ((), (), s32[]{:S(2)}) async-start(), calls=%async_computation.17 | async-start | bytes 2228224
  176.9 4.3 copy-start.7
  180.5 0.7 copy-start.10
  187.0 319.3 %reduce-scatter.27.cloned.1.call-start = ((), (), s32[]{:S(2)}) async-start(), calls=%async_computation.16 | async-start | bytes 2228224
  189.6 42.7 %copy-start.5 = (bf16[256,2048]{1,0:T(8,128)(2,1)S(1)}, bf16[256,2048]{1,0:T(8,128)(2,1)}, u32[]{:S(2)}) copy-start(bf16[256,2048]{1,0:T(8,128)(2,1)} %gather_fusion) | copy-start | bytes 3145732
  193.9 148.7 %copy-start.6 = (bf16[256,2048]{1,0:T(8,128)(2,1)}, bf16[256,2048]{1,0:T(8,128)(2,1)S(1)}, u32[]{:S(2)}) copy-start(bf16[256,2048]{1,0:T(8,128)(2,1)S(1)} %gather_fusion.6) | copy-start | bytes 3145732
  346.0 0.7 copy-start.16
  348.7 2.5 copy-start.12
  351.2 237.1 %reduce-scatter.23.cloned.1.call-start = ((), (), s32[]{:S(2)}) async-start(), calls=%async_computation.14 | async-start | bytes 2228224
  353.2 2.6 copy-start.14
  355.8 314.3 %reduce-scatter.19.cloned.1.call-start = ((), (), s32[]{:S(2)}) async-start(), calls=%async_computation.12 | async-start | bytes 2228224
  360.2 391.8 %reduce-scatter.25.cloned.1.call-start = ((), (), s32[]{:S(2)}) async-start(), calls=%async_computation.15 | async-start | bytes 2228224
  361.1 2.7 copy-start.8
  363.6 470.3 %reduce-scatter.21.cloned.1.call-start = ((), (), s32[]{:S(2)}) async-start(), calls=%async_computation.13 | async-start | bytes 2228224
  364.5 2.7 copy-start.17
  366.9 625.3 %all-reduce.3.cloned.1.call-start = ((), (), s32[]{:S(2)}) async-start(), calls=%async_computation.18 | async-start | bytes 8388608 | tf_op jit(solution)/shard_map/psum | solution.py:24
  369.5 3.6 copy-start.15
  373.1 2.4 copy-start.4
  373.1 2.4 copy-start.13
  376.3 3.6 copy-start.11
  382.1 3.6 copy-start.9
  385.8 2.4 copy-start.3
  992.2 3.3 copy-start.2
  992.2 4.6 copy-start.1
Sparse Core Ops, SparseCore 0:
  11.2 55.0 all-gather.20
  69.3 52.4 all-gather.18
  124.4 52.4 all-gather.22
  179.8 52.4 all-gather.14
  235.3 52.4 all-gather.12
  290.2 52.4 all-gather.16
  346.9 77.3 reduce-scatter.28
  428.5 77.7 reduce-scatter.26
  510.5 77.6 reduce-scatter.22
  592.3 77.7 reduce-scatter.18
  674.3 77.7 reduce-scatter.24
  756.2 77.7 reduce-scatter.20
  837.2 154.9 all-reduce.2
where the time goes:
time: 1000 us
  waiting for transfers between devices  870 us (87%)
  local copies, waits for them, and re-layouts  65.4 us (7%)
  matrix products  39.4 us (4%)
  between operations  14.3 us (1%)
  other arithmetic  13.1 us (1%)
    unnamed x19, waiting for transfers between devices  429 us
    psum x1, waiting for transfers between devices, group_total(): return lax.psum(partial_value.astype(jnp.bfloat16), 'fsdp')  155 us
    all_gather x2, waiting for transfers between devices, body(): lax.all_gather(gate_w[expert], 'dp', axis=0, tiled=True)  105 us
    all_gather x2, waiting for transfers between devices, body(): lax.all_gather(down_w[expert], 'dp', axis=1, tiled=True)  104 us
    all_gather x2, waiting for transfers between devices, body(): lax.all_gather(up_w[expert], 'dp', axis=0, tiled=True)  77.8 us
    unnamed x54, local copies, waits for them, and re-layouts  28.4 us
  transfers between devices with their start and end apart: 13, of which 13 were waited for; matrix products, arithmetic and copies ran while one was open for 11% of the time, Pallas kernels for 0%

commit v1 on v0

--- a/solution.py
+++ b/solution.py
@@ -37,7 +37,9 @@
         )
         gate_full, up_full, down_full = (
             lax.all_gather(gate_w[expert], "dp", axis=0, tiled=True),
-            lax.all_gather(up_w[expert], "dp", axis=0, tiled=True),
+            jnp.concatenate(
+                lax.all_to_all(jnp.stack([up_w[expert]] * lax.axis_size("dp")), "dp", 0, 0), axis=0
+            ),
             lax.all_gather(down_w[expert], "dp", axis=1, tiled=True),
         )
         slot_input = jnp.take(tokens, slot_token, axis=0) * slot_valid[:, None].astype(tokens.dtype)

time: 1000 us -> 922 us (0.922)
  waiting for transfers between devices: 870 us -> 771 us
  starting transfers between devices: 0.93 us -> 15.3 us
    all_gather x2 -> x0, waiting for transfers between devices: 77.8 us -> none  [body(): lax.all_gather(up_w[expert], 'dp', axis=0, tiled=True)]
    all_gather x2, waiting for transfers between devices: 105 us -> 67.6 us  [body(): lax.all_gather(gate_w[expert], 'dp', axis=0, tiled=True)]
    all_to_all x0 -> x2, waiting for transfers between devices: none -> 14.9 us  [body(): lax.all_to_all(jnp.stack([up_w[expert]] * lax.axis_size('dp')), 'dp', 0, 0)]
    all_to_all x0 -> x2, starting transfers between devices: none -> 14.4 us  [body(): lax.all_to_all(jnp.stack([up_w[expert]] * lax.axis_size('dp')), 'dp', 0, 0)]
    unnamed x19 -> x17, waiting for transfers between devices: 429 us -> 428 us
    unnamed x54 -> x52, local copies, waits for them, and re-layouts: 28.4 us -> 28.4 us
  transfers between devices with their start and end apart: 13 -> 13, of which waited for: 13 -> 12; matrix products, arithmetic and copies ran while one was open for 11% -> 12% of each run, Pallas kernels for 0% -> 0%
where the time goes in v1:
time: 922 us; the launch traced here: 921 us
  waiting for transfers between devices  771 us (84%)
  local copies, waits for them, and re-layouts  67.8 us (7%)
  matrix products  39.8 us (4%)
  starting transfers between devices  15.3 us (2%)
  between operations  14.3 us (2%)
  other arithmetic  13.1 us (1%)
    unnamed x17, waiting for transfers between devices  428 us
    psum x1, waiting for transfers between devices, group_total(): return lax.psum(partial_value.astype(jnp.bfloat16), 'fsdp')  155 us
    all_gather x2, waiting for transfers between devices, body(): lax.all_gather(down_w[expert], 'dp', axis=1, tiled=True)  105 us
    all_gather x2, waiting for transfers between devices, body(): lax.all_gather(gate_w[expert], 'dp', axis=0, tiled=True)  67.6 us
    unnamed x52, local copies, waits for them, and re-layouts  28.4 us
  transfers between devices with their start and end apart: 13, of which 12 were waited for; matrix products, arithmetic and copies ran while one was open for 12% of the time, Pallas kernels for 0%

profile of v1, /device:TPU:4, one launch (start us, length us, event | category | flops | bytes accessed | tf_op | source)
XLA Modules:
  0.0 921.0 jit_solution(7571448398140306365)
XLA Ops:
  7.2 1.8 fusion.35
  9.1 1.7 fusion.34
  11.5 1.0 slice_bitcast_fusion.1
  12.5 1.6 stack.33
  14.1 7.6 all-to-all-start
  24.0 1.9 gather_fusion.1
  26.0 1.4 gather_fusion
  27.4 5.2 gather_fusion.6
  32.6 14.9 %all-to-all-done = bf16[16,128,448]{1,2,0:T(8,128)(2,1)} async-done(((bf16[16,128,448]{1,2,0:T(8,128)(2,1)}), bf16[16,128,448]{1,2,0:T(8,128)(2,1)}, u32[]{:S(2)}, u32[]{:S(2)}) %all-to-all-start) | async-done | bytes 1835040 | tf_op jit(solution)/shard_map/all_to_all | solution.py:41
  47.4 1.6 stack.34
  49.0 6.9 all-to-all-start.1
  55.9 3.0 fusion.8
  59.0 34.3 %all-gather.9.cloned.1.call-done = bf16[1,2048,448]{1,2,0:T(8,128)(2,1)} async-done(((bf16[1,128,448]{1,2,0:T(8,128)(2,1)}), bf16[1,2048,448]{1,2,0:T(8,128)(2,1)}) %all-gather.9.cloned.1.call-update) | async-done | bytes 1835024 | tf_op jit(solution)/shard_map/all_gather | solution.py:39
  93.3 3.1 fusion.22
  96.4 53.5 %all-gather.11.cloned.1.call-done = bf16[1,448,2048]{2,1,0:T(8,128)(2,1)} async-done(((bf16[1,448,128]{2,1,0:T(8,128)(2,1)}), bf16[1,448,2048]{2,1,0:T(8,128)(2,1)}) %all-gather.11.cloned.1.call-update) | async-done | bytes 1835024 | tf_op jit(solution)/shard_map/all_gather | solution.py:43
  149.8 3.7 multiply_convert_fusion.4
  154.2 2.0 convolution_convert_fusion.5
  156.2 3.8 copy.28
  160.3 2.3 gather_fusion.3
  162.6 4.3 gather_fusion.8
  167.1 1.9 gather_fusion.4
  169.1 3.1 fusion.5
  172.2 33.3 %all-gather.13.cloned.1.call-done = bf16[1,2048,448]{1,2,0:T(8,128)(2,1)} async-done(((bf16[1,128,448]{1,2,0:T(8,128)(2,1)}), bf16[1,2048,448]{1,2,0:T(8,128)(2,1)}) %all-gather.13.cloned.1.call-update) | async-done | bytes 1835024 | tf_op jit(solution)/shard_map/all_gather | solution.py:39
  205.5 3.0 fusion.15
  208.5 51.8 %all-gather.15.cloned.1.call-done = bf16[1,448,2048]{2,1,0:T(8,128)(2,1)} async-done(((bf16[1,448,128]{2,1,0:T(8,128)(2,1)}), bf16[1,448,2048]{2,1,0:T(8,128)(2,1)}) %all-gather.15.cloned.1.call-update) | async-done | bytes 1835024 | tf_op jit(solution)/shard_map/all_gather | solution.py:43
  260.3 3.3 multiply_convert_fusion.2
  264.3 2.0 convolution_convert_fusion.4
  266.4 2.4 copy.30
  268.9 0.8 convolution_convert_fusion.1
  269.7 2.5 copy.24
  272.2 0.8 convolution_convert_fusion.3
  273.0 2.4 copy.20
  275.5 0.7 convolution_convert_fusion
  276.3 2.5 copy.26
  278.9 0.7 convolution_convert_fusion.2
  279.7 2.4 copy.22
  282.4 2.3 convolution_multiply_fusion
  284.7 3.6 gather_fusion.5
  288.3 2.3 fusion.13
  290.6 2.2 convolution_add_fusion
  292.9 3.6 gather_fusion.9
  296.5 2.2 convolution_multiply_fusion.1
  298.7 3.6 gather_fusion.2
  302.3 2.3 fusion.20
  304.6 2.2 convolution_add_fusion.1
  306.9 3.6 gather_fusion.7
  310.5 9.4 %fusion.1 = (bf16[512,2048]{1,0:T(8,128)(2,1)}, bf16[512,2048]{1,0:T(8,128)(2,1)}) fusion(f32[512,2048]{1,0:T(8,128)} %gather_fusion.9, f32[512,2048]{1,0:T(8,128)} %gather_fusion.7, pred[512]{0:T(512)(128)(4,1)S(1)} %get-tuple-element.16, pred[512]{0:T(512)(128)(4,1)S(1)} %get-tuple-element.14, pred[512]{0:T(512)(128)(4,1)S(1)} %get-tuple-element.11, ...), kind=kLoop, calls=%fused_computation.12 | loop fusion | flops 12582912 | bytes 20973568 | tf_op jit(solution)/shard_map/convert_element_type | solution.py:24
  319.9 21.9 %reduce-scatter.27.cloned.1.call-done = bf16[128,448]{1,0:T(8,128)(2,1)} async-done(((bf16[2048,448]{1,0:T(8,128)(2,1)}), bf16[128,448]{1,0:T(8,128)(2,1)}) %reduce-scatter.27.cloned.1.call-update) | async-done | bytes 114704
  341.8 1.0 copy.29
  342.8 80.8 %reduce-scatter.29.cloned.1.call-done = bf16[128,448]{1,0:T(8,128)(2,1)} async-done(((bf16[2048,448]{1,0:T(8,128)(2,1)}), bf16[128,448]{1,0:T(8,128)(2,1)}) %reduce-scatter.29.cloned.1.call-update) | async-done | bytes 114704
  423.6 1.0 copy.31
  424.7 80.9 %reduce-scatter.23.cloned.1.call-done = bf16[128,448]{1,0:T(8,128)(2,1)} async-done(((bf16[2048,448]{1,0:T(8,128)(2,1)}), bf16[128,448]{1,0:T(8,128)(2,1)}) %reduce-scatter.23.cloned.1.call-update) | async-done | bytes 114704
  505.6 1.0 copy.25
  506.7 80.9 %reduce-scatter.19.cloned.1.call-done = bf16[128,448]{1,0:T(8,128)(2,1)} async-done(((bf16[2048,448]{1,0:T(8,128)(2,1)}), bf16[128,448]{1,0:T(8,128)(2,1)}) %reduce-scatter.19.cloned.1.call-update) | async-done | bytes 114704
  587.6 1.0 copy.21
  588.6 80.9 %reduce-scatter.25.cloned.1.call-done = bf16[128,448]{1,0:T(8,128)(2,1)} async-done(((bf16[2048,448]{1,0:T(8,128)(2,1)}), bf16[128,448]{1,0:T(8,128)(2,1)}) %reduce-scatter.25.cloned.1.call-update) | async-done | bytes 114704
  669.6 1.0 copy.27
  670.6 80.8 %reduce-scatter.21.cloned.1.call-done = bf16[128,448]{1,0:T(8,128)(2,1)} async-done(((bf16[2048,448]{1,0:T(8,128)(2,1)}), bf16[128,448]{1,0:T(8,128)(2,1)}) %reduce-scatter.21.cloned.1.call-update) | async-done | bytes 114704
  751.4 1.0 copy.23
  752.5 0.7 pad_maximum_fusion.2
  753.2 0.7 pad_maximum_fusion.1
  754.6 155.2 %all-reduce.3.cloned.1.call-done = (bf16[512,2048]{1,0:T(8,128)(2,1)}, bf16[512,2048]{1,0:T(8,128)(2,1)}) async-done(((bf16[512,2048]{1,0:T(8,128)(2,1)}, bf16[512,2048]{1,0:T(8,128)(2,1)}), (bf16[512,2048]{1,0:T(8,128)(2,1)}, bf16[512,2048]{1,0:T(8,128)(2,1)})) %all-reduce.3.cloned.1.call-update) | async-done | bytes 4194320 | tf_op jit(solution)/shard_map/psum | solution.py:24
  909.8 3.3 copy.52
  913.1 1.3 copy.53
  (91 shorter events, 6.3 us)
Async XLA Ops:
  7.2 18.8 %copy-start = (bf16[512,2048]{1,0:T(8,128)(2,1)S(1)}, bf16[512,2048]{1,0:T(8,128)(2,1)}, u32[]{:S(2)}) copy-start(bf16[512,2048]{1,0:T(8,128)(2,1)} %param.13) | copy-start | bytes 6291460
  7.2 86.1 %all-gather.9.cloned.1.call-start = ((), (), s32[]{:S(2)}) async-start(), calls=%async_computation.8 | async-start | bytes 1949696 | tf_op jit(solution)/shard_map/all_gather | solution.py:39
  9.0 140.8 %all-gather.11.cloned.1.call-start = ((), (), s32[]{:S(2)}) async-start(), calls=%async_computation.9 | async-start | bytes 1949696 | tf_op jit(solution)/shard_map/all_gather | solution.py:43
  10.8 194.7 %all-gather.13.cloned.1.call-start = ((), (), s32[]{:S(2)}) async-start(), calls=%async_computation.10 | async-start | bytes 1949696 | tf_op jit(solution)/shard_map/all_gather | solution.py:39
  14.1 8.2 copy-start.17
  14.1 9.9 %copy-start.18 = (f32[512,2]{0,1:T(2,128)S(1)}, f32[512,2]{0,1:T(2,128)}, u32[]{:S(2)}) copy-start(f32[512,2]{0,1:T(2,128)} %param.15) | copy-start | bytes 12292
  14.1 33.4 %all-to-all-start = ((bf16[16,128,448]{1,2,0:T(8,128)(2,1)}), bf16[16,128,448]{1,2,0:T(8,128)(2,1)}, u32[]{:S(2)}, u32[]{:S(2)}) async-start(bf16[16,128,448]{1,2,0:T(8,128)(2,1)} %stack.33), calls=%async_computation | async-start | bytes 3670016 | tf_op jit(solution)/shard_map/all_to_all | solution.py:41
  21.7 238.7 %all-gather.15.cloned.1.call-start = ((), (), s32[]{:S(2)}) async-start(), calls=%async_computation.11 | async-start | bytes 1949696 | tf_op jit(solution)/shard_map/all_gather | solution.py:43
  49.0 120.1 %all-to-all-start.1 = ((bf16[16,128,448]{1,2,0:T(8,128)(2,1)}), bf16[16,128,448]{1,2,0:T(8,128)(2,1)}, u32[]{:S(2)}, u32[]{:S(2)}) async-start(bf16[16,128,448]{1,2,0:T(8,128)(2,1)} %stack.34), calls=%async_computation.1 | async-start | bytes 3670016 | tf_op jit(solution)/shard_map/all_to_all | solution.py:41
  55.9 285.9 %reduce-scatter.27.cloned.1.call-start = ((), (), s32[]{:S(2)}) async-start(), calls=%async_computation.16 | async-start | bytes 2228224
  149.8 4.3 copy-start.5
  153.5 0.7 copy-start.9
  160.0 263.6 %reduce-scatter.29.cloned.1.call-start = ((), (), s32[]{:S(2)}) async-start(), calls=%async_computation.17 | async-start | bytes 2228224
  162.6 6.5 copy-start.3
  166.9 93.4 %copy-start.6 = (bf16[256,2048]{1,0:T(8,128)(2,1)}, bf16[256,2048]{1,0:T(8,128)(2,1)S(1)}, u32[]{:S(2)}) copy-start(bf16[256,2048]{1,0:T(8,128)(2,1)S(1)} %gather_fusion.8) | copy-start | bytes 3145732
  263.7 0.7 copy-start.15
  268.8 236.8 %reduce-scatter.23.cloned.1.call-start = ((), (), s32[]{:S(2)}) async-start(), calls=%async_computation.14 | async-start | bytes 2228224
  269.6 2.6 copy-start.7
  272.2 315.4 %reduce-scatter.19.cloned.1.call-start = ((), (), s32[]{:S(2)}) async-start(), calls=%async_computation.12 | async-start | bytes 2228224
  273.0 2.5 copy-start.4
  273.0 2.5 copy-start.11
  275.5 394.1 %reduce-scatter.25.cloned.1.call-start = ((), (), s32[]{:S(2)}) async-start(), calls=%async_computation.15 | async-start | bytes 2228224
  276.3 2.6 copy-start.13
  278.8 472.6 %reduce-scatter.21.cloned.1.call-start = ((), (), s32[]{:S(2)}) async-start(), calls=%async_computation.13 | async-start | bytes 2228224
  279.7 2.7 copy-start.16
  282.1 627.7 %all-reduce.3.cloned.1.call-start = ((), (), s32[]{:S(2)}) async-start(), calls=%async_computation.18 | async-start | bytes 8388608 | tf_op jit(solution)/shard_map/psum | solution.py:24
  284.7 3.6 copy-start.14
  288.3 2.3 copy-start.12
  292.9 3.6 copy-start.10
  298.7 3.6 copy-start.8
  909.8 3.3 copy-start.2
  909.8 4.6 copy-start.1
Sparse Core Ops, SparseCore 0:
  11.1 82.1 all-gather.8
  96.4 53.3 all-gather.10
  153.0 52.4 all-gather.12
  207.9 52.4 all-gather.14
  264.4 77.3 reduce-scatter.26
  345.9 77.7 reduce-scatter.28
  427.9 77.7 reduce-scatter.22
  509.9 77.7 reduce-scatter.18
  591.8 77.6 reduce-scatter.24
  673.6 77.7 reduce-scatter.20
  754.7 155.0 all-reduce.2
